TPU v7x, 32 devices: a whole 2x2x4 slice. The times are simulated.
32 devices in a mesh: grp: 2 (over y), row: 4 (over z), col: 2 (over x), rep: 2 (over core).
Axes of the slice: x: 2, y: 2, z: 4, core: 2. Of those that a mesh axis runs over, the one named last changes fastest.
Arguments:
- shard_rows: bfloat16 [11520, 512], P(('grp', 'row', 'col', 'rep')), parts along dimension 0, may hold values from -24 to 24
- row_position: int32 [11520], P(('grp', 'row', 'col', 'rep')), parts along dimension 0, may hold values from 0 to 3071, as said below
- shard_count: int32 [32], P(('grp', 'row', 'col', 'rep')), parts along dimension 0, may hold values from 1 to 360, as said below
Outputs:
- max_similarity: float32 [6144], P(('grp', 'row', 'col', 'rep')), parts along dimension 0
There are 2 independent parts, one for each index of `grp`. A program takes and returns all parts, laid end to end along the dimension named above; each array names one. Nothing has to cross between parts.
Inputs may be any that keep to these rules, and one draw needn't show every extreme that they name: `row_position`: row j of shard s is used when j < shard_count[s]; the used rows of all shards hold every position 0 to 3071 once, unused rows hold arbitrary positions. At most 24 used rows of one shard have positions in one aligned run of 192 positions, and some shard reaches 24. `shard_count`: the counts sum to 3072.
All inputs are finite; a program needn't handle non-finite values.
Results may differ from a plain program's by a relative error of at most 0.00063.
Values may be sent and summed in bfloat16 or wider, within the bound.
A program may use at most 64 MiB of HBM per device.

v0:
```python
import math

import jax
import jax.numpy as jnp
from jax import lax
from jax.sharding import PartitionSpec as P

OWN = 192


def normalize(owned_rows):
    widened = owned_rows.astype(jnp.float32)
    return (widened / jnp.sqrt(jnp.sum(widened * widened, 1, keepdims=True) + 1e-06)).astype(
        jnp.bfloat16
    )


def body(shard_rows, row_position, shard_count):
    row_devices = lax.axis_size("row")
    cross_devices = lax.axis_size(("col", "rep"))
    all_shards = row_devices * cross_devices
    per_owner = OWN
    owner_load = max(1, per_owner // all_shards)
    slot_count = 2 * owner_load
    block_rows = per_owner * cross_devices
    capacity, feature = shard_rows.shape
    row_place = lax.axis_index("row")
    cross_place = lax.axis_index(("col", "rep"))
    is_used = jnp.arange(capacity) < shard_count[0]
    position = jnp.where(is_used, row_position, 0)
    owner_first = position // per_owner
    one_hot = jnp.logical_and(
        owner_first[:, None] == jnp.arange(all_shards)[None, :], is_used[:, None]
    ).astype(jnp.int32)
    ranking = jnp.sum(jnp.cumsum(one_hot, 0) * one_hot, 1) - 1
    target = jnp.where(is_used, owner_first * slot_count + ranking, all_shards * slot_count)
    packed = (
        jnp.zeros((all_shards * slot_count, feature), shard_rows.dtype)
        .at[target]
        .set(shard_rows, mode="drop")
    )
    placed = (
        jnp.full((all_shards * slot_count,), -1, jnp.int32).at[target].set(position, mode="drop")
    )
    first_packed = packed.reshape(row_devices, cross_devices, slot_count, feature)
    first_placed = placed.reshape(row_devices, cross_devices, slot_count)
    own_offset = row_place * block_rows + cross_place * per_owner
    received = (
        lax.all_to_all(
            lax.all_to_all(first_packed, "row", split_axis=0, concat_axis=0, tiled=True),
            ("col", "rep"),
            split_axis=1,
            concat_axis=1,
            tiled=True,
        ),
        lax.all_to_all(
            lax.all_to_all(first_placed, "row", split_axis=0, concat_axis=0, tiled=True),
            ("col", "rep"),
            split_axis=1,
            concat_axis=1,
            tiled=True,
        ),
    )
    flat_rows = received[0].reshape(-1, feature)
    flat_places = received[1].reshape(-1)
    local_index = jnp.where(flat_places >= 0, flat_places - own_offset, per_owner)
    owned_rows = (
        jnp.zeros((per_owner, feature), flat_rows.dtype).at[local_index].set(flat_rows, mode="drop")
    )
    row_owned = normalize(owned_rows)
    row_block = lax.all_gather(row_owned, ("col", "rep"), axis=0, tiled=True)
    column_index = jnp.arange(block_rows)
    column_block = lax.all_gather(row_owned, "row", axis=0, tiled=True)
    column_places = (
        column_index // per_owner * block_rows + cross_place * per_owner + column_index % per_owner
    )
    row_step = math.gcd(block_rows, 512)
    column_step = math.gcd(block_rows, 1024)

    def row_maxima(inputs):
        row_tile, row_start = inputs
        row_global = row_place * block_rows + row_start + jnp.arange(row_step)
        running = jnp.full((row_step,), -4.0, jnp.float32)
        for column_turn in range(block_rows // column_step):
            column_tile = column_block[column_turn * column_step : (column_turn + 1) * column_step]
            scores = jnp.einsum(
                "rd,cd->rc", row_tile, column_tile, preferred_element_type=jnp.float32
            )
            column_global = column_places[
                column_turn * column_step : (column_turn + 1) * column_step
            ]
            scores = jnp.where(row_global[:, None] == column_global[None, :], -4.0, scores)
            running = jnp.maximum(running, jnp.max(scores, 1))
        return running

    starts = jnp.arange(block_rows // row_step, dtype=jnp.int32) * row_step
    maxima = lax.map(row_maxima, (row_block.reshape(-1, row_step, feature), starts)).reshape(
        block_rows
    )
    combined = lax.pmax(maxima, ("col", "rep"))
    return lax.dynamic_slice_in_dim(combined, cross_place * per_owner, per_owner)


def solution(mesh):
    return jax.shard_map(
        body,
        mesh=mesh,
        in_specs=(
            P(("grp", "row", "col", "rep"), None),
            P(("grp", "row", "col", "rep")),
            P(("grp", "row", "col", "rep")),
        ),
        out_specs=P(("grp", "row", "col", "rep")),
        check_vma=False,
    )
```

profile of v0, /device:TPU:0, one launch (start us, length us, event | category | flops | bytes accessed | tf_op | source)
XLA Modules:
  0.0 92.6 jit_solution(1535740901777857113)
XLA Ops:
  0.7 0.0 copy-start
  0.7 0.7 copy-done
  1.4 0.9 reduce-window.6
  2.3 0.2 slice_reduce_fusion
  2.5 0.1 bitcast_bitcast_fusion
  2.6 2.9 %scatter_custom_fusion = s32[384]{0:T(512)S(1)} fusion(s32[360]{0:T(512)S(1)} %compare_select_fusion.1, s32[360]{0:T(512)S(1)} %get-tuple-element.104, s32[]{:T(128)} %constant.84.clone.1), kind=kCustom, calls=%fused_computation.67 | custom fusion | bytes 1540 | tf_op jit(solution)/shard_map/scatter | solution.py:43
  5.5 0.7 reshape.115
  6.2 6.3 %all-to-all-start = ((s32[4,4,24]{2,1,0:T(4,128)}), s32[4,4,24]{2,1,0:T(4,128)S(1)}, u32[]{:S(2)}, u32[]{:S(2)}) async-start(s32[4,4,24]{2,1,0:T(4,128)} %reshape.115), calls=%async_computation | async-start | bytes 16384 | tf_op jit(solution)/shard_map/all_to_all | solution.py:57
  12.6 3.0 %scatter_custom_fusion.1 = bf16[384,512]{1,0:T(8,128)(2,1)} fusion(s32[360]{0:T(512)S(1)} %compare_select_fusion.1, bf16[360,512]{1,0:T(8,128)(2,1)} %param.5, bf16[]{:T(256)} %constant.83.clone.1), kind=kCustom, calls=%fused_computation.27 | custom fusion | bytes 393728 | tf_op jit(solution)/shard_map/scatter | solution.py:40
  15.6 2.6 %all-to-all-done = s32[4,4,24]{2,1,0:T(4,128)S(1)} async-done(((s32[4,4,24]{2,1,0:T(4,128)}), s32[4,4,24]{2,1,0:T(4,128)S(1)}, u32[]{:S(2)}, u32[]{:S(2)}) %all-to-all-start) | async-done | bytes 1568 | tf_op jit(solution)/shard_map/all_to_all | solution.py:57
  18.2 3.5 %all-to-all-start.2 = ((bf16[4,4,24,512]{3,2,1,0:T(8,128)(2,1)}), bf16[4,4,24,512]{3,2,1,0:T(8,128)(2,1)S(1)}, u32[]{:S(2)}, u32[]{:S(2)}) async-start(bf16[4,4,24,512]{3,2,1,0:T(8,128)(2,1)} %bitcast.5), calls=%async_computation.2 | async-start | bytes 786432 | tf_op jit(solution)/shard_map/all_to_all | solution.py:50
  21.6 0.6 copy.17
  22.2 9.9 %all-to-all-done.2 = bf16[4,4,24,512]{3,2,1,0:T(8,128)(2,1)S(1)} async-done(((bf16[4,4,24,512]{3,2,1,0:T(8,128)(2,1)}), bf16[4,4,24,512]{3,2,1,0:T(8,128)(2,1)S(1)}, u32[]{:S(2)}, u32[]{:S(2)}) %all-to-all-start.2) | async-done | bytes 393248 | tf_op jit(solution)/shard_map/all_to_all | solution.py:50
  32.1 3.2 %all-to-all-start.1 = ((s32[4,4,24]{2,0,1:T(4,128)}), s32[4,4,24]{2,0,1:T(4,128)S(1)}, u32[]{:S(2)}, u32[]{:S(2)}) async-start(s32[4,4,24]{2,0,1:T(4,128)} %copy.17), calls=%async_computation.1 | async-start | bytes 16384 | tf_op jit(solution)/shard_map/all_to_all | solution.py:56
  35.4 0.8 copy.19
  36.2 3.0 %all-to-all-done.1 = s32[4,4,24]{2,0,1:T(4,128)S(1)} async-done(((s32[4,4,24]{2,0,1:T(4,128)}), s32[4,4,24]{2,0,1:T(4,128)S(1)}, u32[]{:S(2)}, u32[]{:S(2)}) %all-to-all-start.1) | async-done | bytes 1568 | tf_op jit(solution)/shard_map/all_to_all | solution.py:56
  39.1 3.5 %all-to-all-start.3 = ((bf16[4,4,24,512]{3,2,0,1:T(8,128)(2,1)}), bf16[4,4,24,512]{3,2,0,1:T(8,128)(2,1)S(1)}, u32[]{:S(2)}, u32[]{:S(2)}) async-start(bf16[4,4,24,512]{3,2,0,1:T(8,128)(2,1)} %copy.19), calls=%async_computation.3 | async-start | bytes 786432 | tf_op jit(solution)/shard_map/all_to_all | solution.py:49
  42.6 0.1 select_n.78
  42.7 7.3 %all-to-all-done.3 = bf16[4,4,24,512]{3,2,0,1:T(8,128)(2,1)S(1)} async-done(((bf16[4,4,24,512]{3,2,0,1:T(8,128)(2,1)}), bf16[4,4,24,512]{3,2,0,1:T(8,128)(2,1)S(1)}, u32[]{:S(2)}, u32[]{:S(2)}) %all-to-all-start.3) | async-done | bytes 393248 | tf_op jit(solution)/shard_map/all_to_all | solution.py:49
  50.0 2.0 %scatter_custom_fusion.2 = bf16[192,512]{1,0:T(8,128)(2,1)S(1)} fusion(s32[384]{0:T(512)S(1)} %fusion.35, bf16[384,512]{1,0:T(8,128)(2,1)S(1)} %bitcast.40, bf16[]{:T(256)} %constant.83.clone.1), kind=kCustom, calls=%fused_computation.29 | custom fusion | bytes 196610 | tf_op jit(solution)/shard_map/scatter | solution.py:68
  52.0 0.1 fusion.15
  52.2 0.1 fusion.16
  52.3 18.0 %all_gather.7 = bf16[768,512]{1,0:T(8,128)(2,1)S(1)} all-gather(bf16[192,512]{1,0:T(8,128)(2,1)S(1)} %fusion.16), channel_id=1, replica_groups=mesh['grp'=2,'row'=4,'col'=2,'rep'=2] {'row'}, dimensions={0}, use_global_device_ids=true | all-gather | bytes 983040 | tf_op jit(solution)/shard_map/all_gather | solution.py:73
  70.3 7.5 %all_gather.6 = bf16[768,512]{1,0:T(8,128)(2,1)S(1)} all-gather(bf16[192,512]{1,0:T(8,128)(2,1)S(1)} %fusion.16), channel_id=1, replica_groups=mesh['grp'=2,'row'=4,'col'=2,'rep'=2] {'col','rep'}, dimensions={0}, use_global_device_ids=true | all-gather | bytes 983040 | tf_op jit(solution)/shard_map/all_gather | solution.py:71
  77.8 6.9 %while.12 = (s32[]{:T(128)}, f32[3,256]{1,0:T(4,128)S(1)}, s32[3]{0:T(128)S(1)}, s32[]{:T(128)}, s32[768]{0:T(1024)S(1)}, /*index=5*/bf16[3,256,512]{2,1,0:T(8,1...) while((s32[]{:T(128)}, f32[3,256]{1,0:T(4,128)S(1)}, s32[3]{0:T(128)S(1)}, s32[]{:T(128)}, ...), condition=%wide.region_11.12_spmd, body=%wide.region_7.11_spmd.sunk | while | flops 201916672 | bytes 1595529 | solution.py:97
  77.8 0.7 dynamic_slice.35
  79.1 0.3 fusion.58
  79.4 0.3 fusion.57
  79.7 0.3 fusion.56
  80.1 0.7 dynamic_slice.35
  81.4 0.3 fusion.58
  81.7 0.3 fusion.57
  82.0 0.3 fusion.56
  82.3 0.7 dynamic_slice.35
  83.7 0.3 fusion.58
  84.0 0.3 fusion.57
  84.3 0.3 fusion.56
  84.6 7.3 %pmax.7 = f32[768]{0:T(1024)S(1)} all-reduce(f32[768]{0:T(1024)S(1)} %reshape.119), channel_id=1, replica_groups=mesh['grp'=2,'row'=4,'col'=2,'rep'=2] {'col','rep'}, use_global_device_ids=true, to_apply=%region_12.13 | all-reduce | flops 768 | bytes 6144 | tf_op jit(solution)/shard_map/pmax | solution.py:100
  91.9 0.6 dynamic_slice.15
  (25 shorter events, 0.4 us)
Async XLA Ops:
  0.7 0.7 copy-start
  6.2 11.9 %all-to-all-start = ((s32[4,4,24]{2,1,0:T(4,128)}), s32[4,4,24]{2,1,0:T(4,128)S(1)}, u32[]{:S(2)}, u32[]{:S(2)}) async-start(s32[4,4,24]{2,1,0:T(4,128)} %reshape.115), calls=%async_computation | async-start | bytes 16384 | tf_op jit(solution)/shard_map/all_to_all | solution.py:57
  18.2 14.0 %all-to-all-start.2 = ((bf16[4,4,24,512]{3,2,1,0:T(8,128)(2,1)}), bf16[4,4,24,512]{3,2,1,0:T(8,128)(2,1)S(1)}, u32[]{:S(2)}, u32[]{:S(2)}) async-start(bf16[4,4,24,512]{3,2,1,0:T(8,128)(2,1)} %bitcast.5), calls=%async_computation.2 | async-start | bytes 786432 | tf_op jit(solution)/shard_map/all_to_all | solution.py:50
  32.1 7.0 %all-to-all-start.1 = ((s32[4,4,24]{2,0,1:T(4,128)}), s32[4,4,24]{2,0,1:T(4,128)S(1)}, u32[]{:S(2)}, u32[]{:S(2)}) async-start(s32[4,4,24]{2,0,1:T(4,128)} %copy.17), calls=%async_computation.1 | async-start | bytes 16384 | tf_op jit(solution)/shard_map/all_to_all | solution.py:56
  39.1 10.9 %all-to-all-start.3 = ((bf16[4,4,24,512]{3,2,0,1:T(8,128)(2,1)}), bf16[4,4,24,512]{3,2,0,1:T(8,128)(2,1)S(1)}, u32[]{:S(2)}, u32[]{:S(2)}) async-start(bf16[4,4,24,512]{3,2,0,1:T(8,128)(2,1)} %copy.19), calls=%async_computation.3 | async-start | bytes 786432 | tf_op jit(solution)/shard_map/all_to_all | solution.py:49
where the time goes:
time: 93.1 us; the launch traced here: 92.6 us
  blocking collectives  32.8 us (35%)
  waiting for transfers between devices  22.7 us (24%)
  starting transfers between devices  16.5 us (18%)
  local copies, waits for them, and re-layouts  13.7 us (15%)
  matrix products  2.53 us (3%)
  loops' own time  2.18 us (2%)
  other arithmetic  1.38 us (1%)
    all_gather x1, blocking collectives, body(): column_block = lax.all_gather(row_owned, 'row', axis=0, tiled=True)  18 us
    all_to_all x1, waiting for transfers between devices, body(): lax.all_to_all(first_packed, 'row', split_axis=0, concat_axis=0, tiled=True)  9.87 us
    all_gather x1, blocking collectives, body(): row_block = lax.all_gather(row_owned, ('col', 'rep'), axis=0, tiled=True)  7.46 us
    pmax x1, blocking collectives, body(): combined = lax.pmax(maxima, ('col', 'rep'))  7.28 us
    all_to_all x1, waiting for transfers between devices, body(): lax.all_to_all(lax.all_to_all(first_packed, 'row', split_axis=0, concat_a...  7.27 us
    all_to_all x1, starting transfers between devices, body(): lax.all_to_all(first_placed, 'row', split_axis=0, concat_axis=0, tiled=True)  6.32 us
    all_to_all x1, starting transfers between devices, body(): lax.all_to_all(first_packed, 'row', split_axis=0, concat_axis=0, tiled=True)  3.46 us
    all_to_all x1, starting transfers between devices, body(): lax.all_to_all(lax.all_to_all(first_packed, 'row', split_axis=0, concat_a...  3.46 us
  transfers between devices with their start and end apart: 4, of which 4 were waited for; matrix products, arithmetic and copies ran while one was open for 5% of the time, Pallas kernels for 0%

commit v1 on v0

--- a/solution.py
+++ b/solution.py
@@ -1,8 +1,11 @@
+import functools
 import math
 
 import jax
 import jax.numpy as jnp
 from jax import lax
+from jax.experimental import pallas as pl
+from jax.experimental.pallas import tpu as pltpu
 from jax.sharding import PartitionSpec as P
 
 OWN = 192
@@ -101,9 +104,364 @@
     return lax.dynamic_slice_in_dim(combined, cross_place * per_owner, per_owner)
 
 
+FLOOR = -8.0
+LANES = 128
+SLOTS = 10
+
+
+def line_kernel(
+    capacity, sent, padded, chunks,
+    rows_ref, place_ref, out_ref,
+    buf, places, row_acc, col_acc, row_bias, col_bias, result, gathered, final_acc,
+    send_sem, recv_sem, place_send, place_recv, final_send, final_recv,
+):
+    z, x, c = lax.axis_index("row"), lax.axis_index("col"), lax.axis_index("rep")
+    me = z * 4 + x * 2 + c
+    inner = jnp.logical_and(z >= 1, z <= 2)
+    low = z <= 1
+    leads = c == z - 1
+    rank = (z - 1) * 4 + x * 2 + c
+
+    def where_is(device):
+        return {"row": device // 4, "col": (device // 2) % 2, "rep": device % 2}
+
+    def at(zz, xx, cc):
+        return {"row": zz, "col": xx, "rep": cc}
+
+    def line_z(turn):
+        ahead = (1, 0, 2, 3)[turn]
+        return jnp.where(low, ahead, 3 - ahead)
+
+    barrier = pltpu.get_barrier_semaphore()
+    for step in range(1, 16):
+        pl.semaphore_signal(
+            barrier, inc=1, device_id=where_is((me + step) % 16), device_id_type=pl.DeviceIdType.MESH
+        )
+
+    widened = rows_ref[...].astype(jnp.float32)
+    scale = jnp.sqrt(jnp.sum(widened * widened, 1, keepdims=True) + 1e-06)
+    buf[0, :capacity] = (widened / scale).astype(jnp.bfloat16)
+    if padded > capacity:
+        buf[0, capacity:] = jnp.zeros((padded - capacity, buf.shape[2]), jnp.bfloat16)
+    places[me] = place_ref[...]
+
+    @pl.when(inner)
+    def _():
+        if padded > sent:
+            for slot in range(1, SLOTS):
+                buf[slot, sent:] = jnp.zeros((padded - sent, buf.shape[2]), jnp.bfloat16)
+        row_acc[...] = jnp.full(row_acc.shape, FLOOR, jnp.float32)
+        col_acc[...] = jnp.full(col_acc.shape, FLOOR, jnp.float32)
+        result[...] = jnp.full(result.shape, FLOOR, jnp.float32)
+
+    pl.semaphore_wait(barrier, 15)
+
+    def copy(src, dst, kind, k, device):
+        begin, count = chunks[k]
+        return pltpu.make_async_remote_copy(
+            src_ref=buf.at[src, pl.ds(begin, count)],
+            dst_ref=buf.at[dst, pl.ds(begin, count)],
+            send_sem=send_sem.at[kind, k],
+            recv_sem=recv_sem.at[dst, k],
+            device_id=device,
+            device_id_type=pl.DeviceIdType.MESH,
+        )
+
+    every = range(len(chunks))
+    inward = at(jnp.where(low, 1, 2), x, c)
+    peer = at(3 - z, x, c)
+    sister = at(z, x, 1 - c)
+    across = at(z, 1, c)
+
+    def arrived(slot, k):
+        copy(slot, slot, 0, k, sister).wait_recv()
+
+    @pl.when(jnp.logical_not(inner))
+    def _():
+        for k in every:
+            copy(0, 1, 0, k, inward).start()
+
+    @pl.when(inner)
+    def _():
+        for k in every:
+            copy(0, 2, 0, k, peer).start()
+
+        @pl.when(jnp.logical_and(leads, x == 0))
+        def _():
+            for k in every:
+                copy(0, 6, 4, k, across).start()
+
+        for k in every:
+            copy(0, 4, 2, k, sister).start()
+
+    def place_copy(step, origin, target):
+        return pltpu.make_async_remote_copy(
+            src_ref=place_ref,
+            dst_ref=places.at[origin],
+            send_sem=place_send.at[step],
+            recv_sem=place_recv.at[step],
+            device_id=where_is(target),
+            device_id_type=pl.DeviceIdType.MESH,
+        )
+
+    for step in range(1, 16):
+        place_copy(step, me, (me + step) % 16).start()
+    for step in range(1, 16):
+        place_copy(step, (me + 16 - step) % 16, (me + step) % 16).wait_recv()
+
+    def pair(a, b, same=False):
+        scores = lax.dot_general(
+            buf[a], buf[b], (((1,), (1,)), ((), ())), preferred_element_type=jnp.float32
+        )
+        if same:
+            row_id = lax.broadcasted_iota(jnp.int32, scores.shape, 0)
+            col_id = lax.broadcasted_iota(jnp.int32, scores.shape, 1)
+            scores = jnp.where(row_id == col_id, FLOOR, scores)
+        bias = row_bias[a]
+        running = None if same else row_acc[a]
+        for j in range(padded // LANES):
+            lanes = slice(j * LANES, (j + 1) * LANES)
+            part = scores[:, lanes]
+            down = jnp.max((part + bias).reshape(padded // 8, 8, LANES), 0)
+            col_acc[b, :, lanes] = jnp.maximum(col_acc[b, :, lanes], down)
+            if not same:
+                running = jnp.maximum(running, part + col_bias[b][:, lanes])
+        if not same:
+            row_acc[a] = running
+
+    def each(begin, end, fn):
+        def step(i, carry):
+            fn(i)
+            return carry
+
+        lax.fori_loop(begin, end, step, 0)
+
+    def finish(slot):
+        found = jnp.max(col_acc[slot], 0, keepdims=True)
+        turned = jnp.max(row_acc[slot].T, 0, keepdims=True)
+        result[pl.ds(slot, 1)] = jnp.maximum(found, turned)
+
+    @pl.when(inner)
+    def _():
+        at_right = x == 1
+        relays = jnp.logical_and(leads, at_right)
+        forwards = jnp.logical_and(leads, x == 0)
+        cross = jnp.where(low, 0, 1)
+        for slot in range(SLOTS):
+            if slot < 4:
+                shard = line_z(slot) * 4 + x * 2 + c
+            elif slot < 6:
+                shard = line_z(slot - 4) * 4 + x * 2 + 1 - c
+            else:
+                shard = line_z(slot - 6) * 4 + cross
+            flat = jnp.where(places[shard] >= 0, 0.0, FLOOR)
+            col_bias[slot] = flat
+            tall = jnp.broadcast_to(flat, (LANES, padded)).T
+            row_bias[slot] = tall
+        pair(0, 0, same=True)
+        for k in every:
+
+            @pl.when(relays)
+            def _():
+                arrived(6, k)
+                copy(6, 6, 4, k, sister).start()
+
+            arrived(1, k)
+            copy(1, 3, 1, k, peer).start()
+            copy(1, 5, 3, k, sister).start()
+
+            @pl.when(forwards)
+            def _():
+                copy(1, 7, 5, k, across).start()
+
+        for k in every:
+            arrived(2, k)
+
+            @pl.when(forwards)
+            def _():
+                copy(2, 8, 6, k, across).start()
+
+        for k in every:
+            arrived(4, k)
+            arrived(5, k)
+        pair(1, 0)
+        pair(1, 1, same=True)
+
+        @pl.when(jnp.logical_not(leads))
+        def _():
+            each(0, 4, lambda i: pair(i // 2, 4 + i % 2))
+
+        first = jnp.where(leads, 0, 2)
+
+        def against(slot):
+            each(first, 4, lambda i: pair(slot, i + 2 * (i // 2)))
+
+        against(2)
+
+        @pl.when(forwards)
+        def _():
+            for k in every:
+                arrived(3, k)
+                copy(3, 9, 7, k, across).start()
+
+        @pl.when(at_right)
+        def _():
+            for j in range(3):
+                for k in every:
+                    if j == 0:
+
+                        @pl.when(jnp.logical_not(leads))
+                        def _():
+                            arrived(6, k)
+
+                    else:
+                        arrived(6 + j, k)
+
+                        @pl.when(leads)
+                        def _():
+                            copy(6 + j, 6 + j, 4 + j, k, sister).start()
+
+                each(0, 3, lambda i: pair(6 + j, i))
+
+        @pl.when(jnp.logical_not(forwards))
+        def _():
+            for k in every:
+                arrived(3, k)
+
+        against(3)
+
+        @pl.when(at_right)
+        def _():
+            each(6, 9, lambda i: pair(i, 3))
+            for k in every:
+                arrived(9, k)
+
+                @pl.when(leads)
+                def _():
+                    copy(9, 9, 7, k, sister).start()
+
+            each(0, 4, lambda i: pair(9, i))
+
+        for slot in range(SLOTS):
+            finish(slot)
+        gathered[rank] = result[...]
+
+    def final_copy(step, target, origin):
+        return pltpu.make_async_remote_copy(
+            src_ref=result,
+            dst_ref=gathered.at[origin],
+            send_sem=final_send.at[step],
+            recv_sem=final_recv.at[origin],
+            device_id=where_is(target),
+            device_id_type=pl.DeviceIdType.MESH,
+        )
+
+    @pl.when(inner)
+    def _():
+        for step in range(1, 16):
+            final_copy(step, (me + step) % 16, rank).start()
+
+    for origin in range(8):
+
+        @pl.when(me != 4 + origin)
+        def _():
+            final_copy(1, (me + 1) % 16, origin).wait_recv()
+
+    mine = lax.broadcasted_iota(jnp.int32, (OWN, LANES), 0) + me * OWN
+    best = jnp.full((OWN, LANES), FLOOR, jnp.float32)
+    for shard in range(16):
+        sz, sx, sc = shard // 4, (shard // 2) % 2, shard % 2
+        value = None
+
+        def add(value, origin, slot):
+            got = gathered[origin, slot : slot + 1]
+            return got if value is None else jnp.maximum(value, got)
+
+        for level in (1, 2):
+            line = (1, 0, 2, 3) if level == 1 else (2, 3, 1, 0)
+            turn = line.index(sz)
+            value = add(value, (level - 1) * 4 + sx * 2 + sc, turn)
+            if turn < 2:
+                value = add(value, (level - 1) * 4 + sx * 2 + 1 - sc, 4 + turn)
+            if sx == 0 and sc == level - 1:
+                for core in (0, 1):
+                    value = add(value, (level - 1) * 4 + 2 + core, 6 + turn)
+        place = places[shard]
+        for j in range(padded // LANES):
+            lanes = slice(j * LANES, (j + 1) * LANES)
+            best = jnp.maximum(best, jnp.where(place[:, lanes] == mine, value[:, lanes], FLOOR))
+    final_acc[:OWN] = best
+    final_acc[OWN:] = jnp.full((final_acc.shape[0] - OWN, LANES), FLOOR, jnp.float32)
+    out_ref[...] = jnp.max(final_acc[...].T, 0, keepdims=True)
+
+    for step in range(1, 16):
+        place_copy(step, me, (me + step) % 16).wait_send()
+
+    @pl.when(jnp.logical_not(inner))
+    def _():
+        for k in every:
+            copy(0, 1, 0, k, inward).wait_send()
+
+    @pl.when(inner)
+    def _():
+        for k in every:
+            copy(0, 2, 0, k, peer).wait_send()
+            copy(1, 3, 1, k, peer).wait_send()
+            copy(0, 4, 2, k, sister).wait_send()
+            copy(1, 5, 3, k, sister).wait_send()
+
+            @pl.when(leads)
+            def _():
+                for turn in range(4):
+                    copy(6 + turn, 6 + turn, 4 + turn, k, sister).wait_send()
+
+        for step in range(1, 16):
+            final_copy(step, (me + step) % 16, rank).wait_send()
+
+
+def line_body(shard_rows, row_position, shard_count):
+    capacity, feature = shard_rows.shape
+    sent = -(-capacity // 16) * 16
+    padded = -(-capacity // LANES) * LANES
+    pieces = 3
+    size = -(-sent // (16 * pieces)) * 16
+    chunks = [(begin, min(size, sent - begin)) for begin in range(0, sent, size)]
+    slot_index = jnp.arange(padded)
+    place = jnp.where(
+        slot_index < shard_count[0], jnp.pad(row_position, (0, padded - capacity)), -1
+    )[None, :]
+    tall = -(-OWN // LANES) * LANES
+    found = pl.pallas_call(
+        functools.partial(line_kernel, capacity, sent, padded, chunks),
+        out_shape=jax.ShapeDtypeStruct((1, tall), jnp.float32),
+        in_specs=[pl.BlockSpec(memory_space=pltpu.VMEM)] * 2,
+        out_specs=pl.BlockSpec(memory_space=pltpu.VMEM),
+        scratch_shapes=[
+            pltpu.VMEM((SLOTS, padded, feature), jnp.bfloat16),
+            pltpu.VMEM((16, 1, padded), jnp.int32),
+            pltpu.VMEM((SLOTS, padded, LANES), jnp.float32),
+            pltpu.VMEM((SLOTS, 8, padded), jnp.float32),
+            pltpu.VMEM((SLOTS, padded, LANES), jnp.float32),
+            pltpu.VMEM((SLOTS, 1, padded), jnp.float32),
+            pltpu.VMEM((16, padded), jnp.float32),
+            pltpu.VMEM((8, 16, padded), jnp.float32),
+            pltpu.VMEM((tall, LANES), jnp.float32),
+            pltpu.SemaphoreType.DMA((8, len(chunks))),
+            pltpu.SemaphoreType.DMA((SLOTS, len(chunks))),
+            pltpu.SemaphoreType.DMA((16,)),
+            pltpu.SemaphoreType.DMA((16,)),
+            pltpu.SemaphoreType.DMA((16,)),
+            pltpu.SemaphoreType.DMA((8,)),
+        ],
+        compiler_params=pltpu.CompilerParams(collective_id=0, has_side_effects=True),
+    )(shard_rows, place)
+    return found[0, :OWN]
+
+
 def solution(mesh):
+    sizes = tuple(mesh.shape[axis] for axis in ("row", "col", "rep"))
     return jax.shard_map(
-        body,
+        line_body if sizes == (4, 2, 2) else body,
         mesh=mesh,
         in_specs=(
             P(("grp", "row", "col", "rep"), None),

time: 93.1 us -> 45.8 us (0.49)
  Pallas kernels: 0 us -> 42.6 us
  blocking collectives: 32.8 us -> 0 us
  waiting for transfers between devices: 22.7 us -> 0 us
  starting transfers between devices: 16.5 us -> 0 us
  local copies, waits for them, and re-layouts: 13.7 us -> 1.8 us
  matrix products: 2.53 us -> 0 us
  loops' own time: 2.18 us -> 0 us
  other arithmetic: 1.38 us -> 0.01 us
    pallas_call x0 -> x1, Pallas kernels: none -> 42.6 us  [line_body(): pl.pallas_call(functools.partial(line_kernel, capacity, sent, padded, chu...]
    all_gather x2 -> x0, blocking collectives: 25.5 us -> none  [the longest x1 18 us: body(): column_block = lax.all_gather(row_owned, 'row', axis=0, tiled=True)]
    all_to_all x4 -> x0, waiting for transfers between devices: 22.7 us -> none  [the longest x1 9.87 us: body(): lax.all_to_all(first_packed, 'row', split_axis=0, concat_axis=0, tiled=True)]
    all_to_all x4 -> x0, starting transfers between devices: 16.5 us -> none  [the longest x1 6.32 us: body(): lax.all_to_all(first_placed, 'row', split_axis=0, concat_axis=0, tiled=True)]
    scatter x3 -> x0, local copies, waits for them, and re-layouts: 7.89 us -> none  [the longest x1 3.02 us: body(): packed = jnp.zeros((all_shards * slot_count, feature), shard_rows.dtype)....]
    pmax x1 -> x0, blocking collectives: 7.28 us -> none  [body(): combined = lax.pmax(maxima, ('col', 'rep'))]
    dynamic_slice x4 -> x0, local copies, waits for them, and re-layouts: 2.63 us -> none  [the longest x3 1.99 us: body(): lax.map(row_maxima, (row_block.reshape(-1, row_step, feature), starts))]
    dot_general x9 -> x0, matrix products: 2.53 us -> none  [row_maxima(): jnp.einsum('rd,cd->rc', row_tile, column_tile, preferred_element_type=jnp...]
  transfers between devices with their start and end apart: 4 -> 0, of which waited for: 4 -> 0; matrix products, arithmetic and copies ran while one was open for 5% -> 0% of each run, Pallas kernels for 0% -> 0%
where the time goes in v1:
time: 45.8 us; the launch traced here: 45.1 us
  Pallas kernels  42.6 us (93%)
  local copies, waits for them, and re-layouts  1.8 us (4%)
  between operations  0.69 us (2%)
    pallas_call x1, Pallas kernels, line_body(): pl.pallas_call(functools.partial(line_kernel, capacity, sent, padded, chu...  42.6 us
    unnamed x5, local copies, waits for them, and re-layouts  1.24 us

profile of v1, /device:TPU:0, one launch (start us, length us, event | category | flops | bytes accessed | tf_op | source)
XLA Modules:
  0.0 45.1 jit_solution(11671584472334154085)
XLA Ops:
  0.0 0.0 copy-start.1
  0.7 0.0 copy-done.1
  0.7 0.6 %broadcast_in_dim.8.place_ref = s32[1,384]{1,0:T(1,128)} reshape(s32[384]{0:T(512)S(1)} %pad_select_fusion) | data formatting | bytes 3072 | tf_op jit(solution)/shard_map/broadcast_in_dim | solution.py:430
  1.3 42.6 %shard_map.37 = f32[1,256]{1,0:T(1,128)} custom-call(bf16[360,512]{1,0:T(8,128)(2,1)} %rows_ref.1, s32[1,384]{1,0:T(1,128)} %broadcast_in_dim.8.place_ref), custom_call_target="tpu_custom_call" | custom-call | tf_op jit(solution)/shard_map/pallas_call | solution.py:434
  43.9 0.0 copy-start
  43.9 0.7 %copy-done = f32[1,256]{1,0:T(1,128)S(1)} copy-done((f32[1,256]{1,0:T(1,128)S(1)}, f32[1,256]{1,0:T(1,128)}, u32[]{:S(2)}) %copy-start) | copy-done | bytes 1048
  44.6 0.6 %copy.6 = f32[192]{0:T(256)} copy(f32[192]{0:T(256)S(1)} %bitcast.4) | data formatting | bytes 1536
  (1 shorter events, 0.0 us)
Async XLA Ops:
  0.0 0.7 %copy-start.1 = (s32[360]{0:T(512)S(1)}, s32[360]{0:T(512)}, u32[]{:S(2)}) copy-start(s32[360]{0:T(512)} %param.4) | copy-start | bytes 4324
  43.9 0.7 %copy-start = (f32[1,256]{1,0:T(1,128)S(1)}, f32[1,256]{1,0:T(1,128)}, u32[]{:S(2)}) copy-start(f32[1,256]{1,0:T(1,128)} %shard_map.37) | copy-start | bytes 3076

commit v2 on v1

--- a/solution.py
+++ b/solution.py
@@ -112,7 +112,7 @@
 def line_kernel(
     capacity, sent, padded, chunks,
     rows_ref, place_ref, out_ref,
-    buf, places, row_acc, col_acc, row_bias, col_bias, result, gathered, final_acc,
+    buf, slot_place, places, row_acc, col_acc, row_bias, col_bias, result, gathered, final_acc,
     send_sem, recv_sem, place_send, place_recv, final_send, final_recv,
 ):
     z, x, c = lax.axis_index("row"), lax.axis_index("col"), lax.axis_index("rep")
@@ -128,22 +128,33 @@
     def at(zz, xx, cc):
         return {"row": zz, "col": xx, "rep": cc}
 
-    def line_z(turn):
-        ahead = (1, 0, 2, 3)[turn]
-        return jnp.where(low, ahead, 3 - ahead)
-
+    sister = at(z, x, 1 - c)
+    across = at(z, 1 - x, c)
+    greeted = [sister, across, at(z, 1 - x, 1 - c)]
     barrier = pltpu.get_barrier_semaphore()
-    for step in range(1, 16):
+
+    def greet(device):
         pl.semaphore_signal(
-            barrier, inc=1, device_id=where_is((me + step) % 16), device_id_type=pl.DeviceIdType.MESH
+            barrier, inc=1, device_id=device, device_id_type=pl.DeviceIdType.MESH
         )
+
+    for device in greeted:
+        greet(device)
+
+    @pl.when(z >= 1)
+    def _():
+        greet(at(z - 1, x, c))
+
+    @pl.when(z <= 2)
+    def _():
+        greet(at(z + 1, x, c))
 
     widened = rows_ref[...].astype(jnp.float32)
     scale = jnp.sqrt(jnp.sum(widened * widened, 1, keepdims=True) + 1e-06)
     buf[0, :capacity] = (widened / scale).astype(jnp.bfloat16)
     if padded > capacity:
         buf[0, capacity:] = jnp.zeros((padded - capacity, buf.shape[2]), jnp.bfloat16)
-    places[me] = place_ref[...]
+    slot_place[0] = place_ref[...]
 
     @pl.when(inner)
     def _():
@@ -154,27 +165,37 @@
         col_acc[...] = jnp.full(col_acc.shape, FLOOR, jnp.float32)
         result[...] = jnp.full(result.shape, FLOOR, jnp.float32)
 
-    pl.semaphore_wait(barrier, 15)
+    @pl.when(inner)
+    def _():
+        pl.semaphore_wait(barrier, 5)
+
+    @pl.when(jnp.logical_not(inner))
+    def _():
+        pl.semaphore_wait(barrier, 4)
 
     def copy(src, dst, kind, k, device):
-        begin, count = chunks[k]
+        if k == len(chunks):
+            src_ref = place_ref if src == 0 else slot_place.at[src]
+            dst_ref = slot_place.at[dst]
+        else:
+            begin, count = chunks[k]
+            src_ref = buf.at[src, pl.ds(begin, count)]
+            dst_ref = buf.at[dst, pl.ds(begin, count)]
         return pltpu.make_async_remote_copy(
-            src_ref=buf.at[src, pl.ds(begin, count)],
-            dst_ref=buf.at[dst, pl.ds(begin, count)],
+            src_ref=src_ref,
+            dst_ref=dst_ref,
             send_sem=send_sem.at[kind, k],
             recv_sem=recv_sem.at[dst, k],
             device_id=device,
             device_id_type=pl.DeviceIdType.MESH,
         )
 
-    every = range(len(chunks))
+    every = [len(chunks)] + list(range(len(chunks)))
     inward = at(jnp.where(low, 1, 2), x, c)
     peer = at(3 - z, x, c)
-    sister = at(z, x, 1 - c)
-    across = at(z, 1, c)
 
     def arrived(slot, k):
-        copy(slot, slot, 0, k, sister).wait_recv()
+        copy(1, slot, 0, k, sister).wait_recv()
 
     @pl.when(jnp.logical_not(inner))
     def _():
@@ -185,29 +206,18 @@
     def _():
         for k in every:
             copy(0, 2, 0, k, peer).start()
-
-        @pl.when(jnp.logical_and(leads, x == 0))
-        def _():
-            for k in every:
-                copy(0, 6, 4, k, across).start()
-
-        for k in every:
+            copy(0, 6, 4, k, across).start()
             copy(0, 4, 2, k, sister).start()
 
-    def place_copy(step, origin, target):
+    def place_copy(step, target, origin):
         return pltpu.make_async_remote_copy(
-            src_ref=place_ref,
+            src_ref=slot_place.at[pl.ds(0, 2)],
             dst_ref=places.at[origin],
             send_sem=place_send.at[step],
-            recv_sem=place_recv.at[step],
+            recv_sem=place_recv.at[origin],
             device_id=where_is(target),
             device_id_type=pl.DeviceIdType.MESH,
         )
-
-    for step in range(1, 16):
-        place_copy(step, me, (me + step) % 16).start()
-    for step in range(1, 16):
-        place_copy(step, (me + 16 - step) % 16, (me + step) % 16).wait_recv()
 
     def pair(a, b, same=False):
         scores = lax.dot_general(
@@ -238,52 +248,31 @@
 
     def finish(slot):
         found = jnp.max(col_acc[slot], 0, keepdims=True)
-        turned = jnp.max(row_acc[slot].T, 0, keepdims=True)
-        result[pl.ds(slot, 1)] = jnp.maximum(found, turned)
-
-    @pl.when(inner)
-    def _():
-        at_right = x == 1
-        relays = jnp.logical_and(leads, at_right)
-        forwards = jnp.logical_and(leads, x == 0)
-        cross = jnp.where(low, 0, 1)
-        for slot in range(SLOTS):
-            if slot < 4:
-                shard = line_z(slot) * 4 + x * 2 + c
-            elif slot < 6:
-                shard = line_z(slot - 4) * 4 + x * 2 + 1 - c
-            else:
-                shard = line_z(slot - 6) * 4 + cross
-            flat = jnp.where(places[shard] >= 0, 0.0, FLOOR)
+        if slot < 4:
+            found = jnp.maximum(found, jnp.max(row_acc[slot].T, 0, keepdims=True))
+        result[slot] = found
+
+    @pl.when(inner)
+    def _():
+        def set_bias(slot):
+            flat = jnp.where(slot_place[slot] >= 0, 0.0, FLOOR)
             col_bias[slot] = flat
-            tall = jnp.broadcast_to(flat, (LANES, padded)).T
-            row_bias[slot] = tall
+            row_bias[slot] = jnp.broadcast_to(flat, (LANES, padded)).T
+
+        set_bias(0)
         pair(0, 0, same=True)
         for k in every:
-
-            @pl.when(relays)
-            def _():
-                arrived(6, k)
-                copy(6, 6, 4, k, sister).start()
-
+            arrived(6, k)
+            copy(6, 8, 6, k, sister).start()
             arrived(1, k)
             copy(1, 3, 1, k, peer).start()
+            copy(1, 7, 5, k, across).start()
             copy(1, 5, 3, k, sister).start()
-
-            @pl.when(forwards)
-            def _():
-                copy(1, 7, 5, k, across).start()
-
-        for k in every:
-            arrived(2, k)
-
-            @pl.when(forwards)
-            def _():
-                copy(2, 8, 6, k, across).start()
-
-        for k in every:
-            arrived(4, k)
-            arrived(5, k)
+        for slot in (2, 4, 5, 8):
+            for k in every:
+                arrived(slot, k)
+        for slot in (1, 2, 4, 5, 6, 8):
+            set_bias(slot)
         pair(1, 0)
         pair(1, 1, same=True)
 
@@ -292,56 +281,41 @@
             each(0, 4, lambda i: pair(i // 2, 4 + i % 2))
 
         first = jnp.where(leads, 0, 2)
+        across_turn = 2 * x
 
         def against(slot):
             each(first, 4, lambda i: pair(slot, i + 2 * (i // 2)))
 
         against(2)
-
-        @pl.when(forwards)
+        arrived(3, len(chunks))
+        places[rank] = slot_place[:2]
+        for step in range(1, 16):
+            place_copy(step, (me + step) % 16, rank).start()
+        each(0, 2, lambda i: pair(across_turn, 6 + 2 * i))
+
+        @pl.when(x == 0)
         def _():
-            for k in every:
-                arrived(3, k)
-                copy(3, 9, 7, k, across).start()
-
-        @pl.when(at_right)
+            each(0, 2, lambda i: pair(1, 6 + 2 * i))
+
+        for k in every:
+            arrived(7, k)
+            copy(7, 9, 7, k, sister).start()
+        set_bias(7)
+        pair(across_turn, 7)
+        for k in every[1:]:
+            arrived(3, k)
+        set_bias(3)
+        against(3)
+
+        @pl.when(x == 1)
         def _():
-            for j in range(3):
-                for k in every:
-                    if j == 0:
-
-                        @pl.when(jnp.logical_not(leads))
-                        def _():
-                            arrived(6, k)
-
-                    else:
-                        arrived(6 + j, k)
-
-                        @pl.when(leads)
-                        def _():
-                            copy(6 + j, 6 + j, 4 + j, k, sister).start()
-
-                each(0, 3, lambda i: pair(6 + j, i))
-
-        @pl.when(jnp.logical_not(forwards))
-        def _():
-            for k in every:
-                arrived(3, k)
-
-        against(3)
-
-        @pl.when(at_right)
-        def _():
-            each(6, 9, lambda i: pair(i, 3))
-            for k in every:
-                arrived(9, k)
-
-                @pl.when(leads)
-                def _():
-                    copy(9, 9, 7, k, sister).start()
-
-            each(0, 4, lambda i: pair(9, i))
-
+            each(0, 2, lambda i: pair(3, 6 + 2 * i))
+
+        pair(across_turn + 1, 7)
+        for k in every:
+            arrived(9, k)
+        set_bias(9)
+        each(0, 2, lambda i: pair(across_turn + i, 9))
         for slot in range(SLOTS):
             finish(slot)
         gathered[rank] = result[...]
@@ -365,6 +339,7 @@
 
         @pl.when(me != 4 + origin)
         def _():
+            place_copy(1, (me + 1) % 16, origin).wait_recv()
             final_copy(1, (me + 1) % 16, origin).wait_recv()
 
     mine = lax.broadcasted_iota(jnp.int32, (OWN, LANES), 0) + me * OWN
@@ -374,7 +349,7 @@
         value = None
 
         def add(value, origin, slot):
-            got = gathered[origin, slot : slot + 1]
+            got = gathered[origin, slot]
             return got if value is None else jnp.maximum(value, got)
 
         for level in (1, 2):
@@ -383,10 +358,12 @@
             value = add(value, (level - 1) * 4 + sx * 2 + sc, turn)
             if turn < 2:
                 value = add(value, (level - 1) * 4 + sx * 2 + 1 - sc, 4 + turn)
-            if sx == 0 and sc == level - 1:
                 for core in (0, 1):
-                    value = add(value, (level - 1) * 4 + 2 + core, 6 + turn)
-        place = places[shard]
+                    origin = (level - 1) * 4 + (1 - sx) * 2 + core
+                    value = add(value, origin, 6 + turn + 2 * (core ^ sc))
+        level = 1 if sz <= 1 else 2
+        turn = ((1, 0) if level == 1 else (2, 3)).index(sz)
+        place = places[(level - 1) * 4 + sx * 2 + sc, turn]
         for j in range(padded // LANES):
             lanes = slice(j * LANES, (j + 1) * LANES)
             best = jnp.maximum(best, jnp.where(place[:, lanes] == mine, value[:, lanes], FLOOR))
@@ -394,9 +371,6 @@
     final_acc[OWN:] = jnp.full((final_acc.shape[0] - OWN, LANES), FLOOR, jnp.float32)
     out_ref[...] = jnp.max(final_acc[...].T, 0, keepdims=True)
 
-    for step in range(1, 16):
-        place_copy(step, me, (me + step) % 16).wait_send()
-
     @pl.when(jnp.logical_not(inner))
     def _():
         for k in every:
@@ -410,12 +384,13 @@
             copy(0, 4, 2, k, sister).wait_send()
             copy(1, 5, 3, k, sister).wait_send()
 
-            @pl.when(leads)
-            def _():
-                for turn in range(4):
-                    copy(6 + turn, 6 + turn, 4 + turn, k, sister).wait_send()
+            copy(0, 6, 4, k, across).wait_send()
+            copy(1, 7, 5, k, across).wait_send()
+            copy(6, 8, 6, k, sister).wait_send()
+            copy(7, 9, 7, k, sister).wait_send()
 
         for step in range(1, 16):
+            place_copy(step, (me + step) % 16, rank).wait_send()
             final_copy(step, (me + step) % 16, rank).wait_send()
 
 
@@ -438,18 +413,19 @@
         out_specs=pl.BlockSpec(memory_space=pltpu.VMEM),
         scratch_shapes=[
             pltpu.VMEM((SLOTS, padded, feature), jnp.bfloat16),
-            pltpu.VMEM((16, 1, padded), jnp.int32),
-            pltpu.VMEM((SLOTS, padded, LANES), jnp.float32),
+            pltpu.VMEM((SLOTS, 1, padded), jnp.int32),
+            pltpu.VMEM((8, 2, 1, padded), jnp.int32),
+            pltpu.VMEM((4, padded, LANES), jnp.float32),
             pltpu.VMEM((SLOTS, 8, padded), jnp.float32),
             pltpu.VMEM((SLOTS, padded, LANES), jnp.float32),
             pltpu.VMEM((SLOTS, 1, padded), jnp.float32),
-            pltpu.VMEM((16, padded), jnp.float32),
-            pltpu.VMEM((8, 16, padded), jnp.float32),
+            pltpu.VMEM((SLOTS, 1, padded), jnp.float32),
+            pltpu.VMEM((8, SLOTS, 1, padded), jnp.float32),
             pltpu.VMEM((tall, LANES), jnp.float32),
-            pltpu.SemaphoreType.DMA((8, len(chunks))),
-            pltpu.SemaphoreType.DMA((SLOTS, len(chunks))),
+            pltpu.SemaphoreType.DMA((8, len(chunks) + 1)),
+            pltpu.SemaphoreType.DMA((SLOTS, len(chunks) + 1)),
             pltpu.SemaphoreType.DMA((16,)),
-            pltpu.SemaphoreType.DMA((16,)),
+            pltpu.SemaphoreType.DMA((8,)),
             pltpu.SemaphoreType.DMA((16,)),
             pltpu.SemaphoreType.DMA((8,)),
         ],

time: 45.8 us -> 36.3 us (0.79); the launches traced: 45.1 us -> 36.2 us
  Pallas kernels: 42.6 us -> 33.7 us
    pallas_call x1, Pallas kernels: 42.6 us -> 33.7 us  [line_body(): pl.pallas_call(functools.partial(line_kernel, capacity, sent, padded, chu...]
where the time goes in v2:
time: 36.3 us; the launch traced here: 36.2 us
  Pallas kernels  33.7 us (93%)
  local copies, waits for them, and re-layouts  1.8 us (5%)
  between operations  0.69 us (2%)
    pallas_call x1, Pallas kernels, line_body(): pl.pallas_call(functools.partial(line_kernel, capacity, sent, padded, chu...  33.7 us
    unnamed x5, local copies, waits for them, and re-layouts  1.24 us

profile of v2, /device:TPU:0, one launch (start us, length us, event | category | flops | bytes accessed | tf_op | source)
XLA Modules:
  0.0 36.2 jit_solution(4015118577952000239)
XLA Ops:
  0.0 0.0 copy-start.1
  0.7 0.0 copy-done.1
  0.7 0.6 %broadcast_in_dim.8.place_ref = s32[1,384]{1,0:T(1,128)} reshape(s32[384]{0:T(512)S(1)} %pad_select_fusion) | data formatting | bytes 3072 | tf_op jit(solution)/shard_map/broadcast_in_dim | solution.py:405
  1.3 33.7 %shard_map.37 = f32[1,256]{1,0:T(1,128)} custom-call(bf16[360,512]{1,0:T(8,128)(2,1)} %rows_ref.1, s32[1,384]{1,0:T(1,128)} %broadcast_in_dim.8.place_ref), custom_call_target="tpu_custom_call" | custom-call | tf_op jit(solution)/shard_map/pallas_call | solution.py:409
  34.9 0.0 copy-start
  34.9 0.7 %copy-done = f32[1,256]{1,0:T(1,128)S(1)} copy-done((f32[1,256]{1,0:T(1,128)S(1)}, f32[1,256]{1,0:T(1,128)}, u32[]{:S(2)}) %copy-start) | copy-done | bytes 1048
  35.6 0.6 %copy.6 = f32[192]{0:T(256)} copy(f32[192]{0:T(256)S(1)} %bitcast.4) | data formatting | bytes 1536
  (1 shorter events, 0.0 us)
Async XLA Ops:
  0.0 0.7 %copy-start.1 = (s32[360]{0:T(512)S(1)}, s32[360]{0:T(512)}, u32[]{:S(2)}) copy-start(s32[360]{0:T(512)} %param.4) | copy-start | bytes 4324
  34.9 0.7 %copy-start = (f32[1,256]{1,0:T(1,128)S(1)}, f32[1,256]{1,0:T(1,128)}, u32[]{:S(2)}) copy-start(f32[1,256]{1,0:T(1,128)} %shard_map.37) | copy-start | bytes 3076

commit v3 on v2

--- a/solution.py
+++ b/solution.py
@@ -111,7 +111,7 @@
 
 def line_kernel(
     capacity, sent, padded, chunks,
-    rows_ref, place_ref, out_ref,
+    rows_ref, raw_ref, count_ref, out_ref,
     buf, slot_place, places, row_acc, col_acc, row_bias, col_bias, result, gathered, final_acc,
     send_sem, recv_sem, place_send, place_recv, final_send, final_recv,
 ):
@@ -154,7 +154,10 @@
     buf[0, :capacity] = (widened / scale).astype(jnp.bfloat16)
     if padded > capacity:
         buf[0, capacity:] = jnp.zeros((padded - capacity, buf.shape[2]), jnp.bfloat16)
-    slot_place[0] = place_ref[...]
+    slot_place[0] = jnp.full((1, padded), -1, jnp.int32)
+    slot_place[0, 0, pl.ds(0, capacity)] = raw_ref[...]
+    slot_id = lax.broadcasted_iota(jnp.int32, (1, padded), 1)
+    slot_place[0] = jnp.where(slot_id < count_ref[0], slot_place[0], -1)
 
     @pl.when(inner)
     def _():
@@ -175,7 +178,7 @@
 
     def copy(src, dst, kind, k, device):
         if k == len(chunks):
-            src_ref = place_ref if src == 0 else slot_place.at[src]
+            src_ref = slot_place.at[src]
             dst_ref = slot_place.at[dst]
         else:
             begin, count = chunks[k]
@@ -239,6 +242,22 @@
         if not same:
             row_acc[a] = running
 
+    def double(a, b):
+        rows = buf[pl.ds(a, 2)].reshape(2 * padded, buf.shape[2])
+        scores = lax.dot_general(
+            rows, buf[b], (((1,), (1,)), ((), ())), preferred_element_type=jnp.float32
+        )
+        for half in range(2):
+            bias = row_bias[a + half]
+            running = row_acc[a + half]
+            for j in range(padded // LANES):
+                lanes = slice(j * LANES, (j + 1) * LANES)
+                part = scores[half * padded : (half + 1) * padded, lanes]
+                down = jnp.max((part + bias).reshape(padded // 8, 8, LANES), 0)
+                col_acc[b, :, lanes] = jnp.maximum(col_acc[b, :, lanes], down)
+                running = jnp.maximum(running, part + col_bias[b][:, lanes])
+            row_acc[a + half] = running
+
     def each(begin, end, fn):
         def step(i, carry):
             fn(i)
@@ -248,7 +267,7 @@
 
     def finish(slot):
         found = jnp.max(col_acc[slot], 0, keepdims=True)
-        if slot < 4:
+        if slot < 8:
             found = jnp.maximum(found, jnp.max(row_acc[slot].T, 0, keepdims=True))
         result[slot] = found
 
@@ -262,46 +281,45 @@
         set_bias(0)
         pair(0, 0, same=True)
         for k in every:
-            arrived(6, k)
-            copy(6, 8, 6, k, sister).start()
             arrived(1, k)
             copy(1, 3, 1, k, peer).start()
-            copy(1, 7, 5, k, across).start()
+            copy(1, 8, 5, k, across).start()
             copy(1, 5, 3, k, sister).start()
-        for slot in (2, 4, 5, 8):
+            arrived(6, k)
+            copy(6, 7, 6, k, sister).start()
+        for slot in (2, 4, 5, 7):
             for k in every:
                 arrived(slot, k)
-        for slot in (1, 2, 4, 5, 6, 8):
+        for slot in (1, 2, 4, 5, 6, 7):
             set_bias(slot)
         pair(1, 0)
         pair(1, 1, same=True)
 
         @pl.when(jnp.logical_not(leads))
         def _():
-            each(0, 4, lambda i: pair(i // 2, 4 + i % 2))
-
-        first = jnp.where(leads, 0, 2)
+            each(0, 2, lambda i: double(4, i))
+
+        first = jnp.where(leads, 0, 1)
         across_turn = 2 * x
 
         def against(slot):
-            each(first, 4, lambda i: pair(slot, i + 2 * (i // 2)))
+            each(first, 2, lambda i: double(4 * i, slot))
 
         against(2)
         arrived(3, len(chunks))
         places[rank] = slot_place[:2]
         for step in range(1, 16):
             place_copy(step, (me + step) % 16, rank).start()
-        each(0, 2, lambda i: pair(across_turn, 6 + 2 * i))
+        each(0, 2 - x, lambda i: double(6, across_turn + i))
+        for k in every:
+            arrived(8, k)
+            copy(8, 9, 7, k, sister).start()
+        set_bias(8)
 
         @pl.when(x == 0)
         def _():
-            each(0, 2, lambda i: pair(1, 6 + 2 * i))
-
-        for k in every:
-            arrived(7, k)
-            copy(7, 9, 7, k, sister).start()
-        set_bias(7)
-        pair(across_turn, 7)
+            double(0, 8)
+
         for k in every[1:]:
             arrived(3, k)
         set_bias(3)
@@ -309,13 +327,13 @@
 
         @pl.when(x == 1)
         def _():
-            each(0, 2, lambda i: pair(3, 6 + 2 * i))
-
-        pair(across_turn + 1, 7)
+            double(6, 3)
+
         for k in every:
             arrived(9, k)
         set_bias(9)
-        each(0, 2, lambda i: pair(across_turn + i, 9))
+        each(jnp.where(x == 0, 9, 8), 10, lambda i: double(across_turn, i))
+
         for slot in range(SLOTS):
             finish(slot)
         gathered[rank] = result[...]
@@ -360,7 +378,7 @@
                 value = add(value, (level - 1) * 4 + sx * 2 + 1 - sc, 4 + turn)
                 for core in (0, 1):
                     origin = (level - 1) * 4 + (1 - sx) * 2 + core
-                    value = add(value, origin, 6 + turn + 2 * (core ^ sc))
+                    value = add(value, origin, 6 + 2 * turn + (core ^ sc))
         level = 1 if sz <= 1 else 2
         turn = ((1, 0) if level == 1 else (2, 3)).index(sz)
         place = places[(level - 1) * 4 + sx * 2 + sc, turn]
@@ -369,7 +387,7 @@
             best = jnp.maximum(best, jnp.where(place[:, lanes] == mine, value[:, lanes], FLOOR))
     final_acc[:OWN] = best
     final_acc[OWN:] = jnp.full((final_acc.shape[0] - OWN, LANES), FLOOR, jnp.float32)
-    out_ref[...] = jnp.max(final_acc[...].T, 0, keepdims=True)
+    out_ref[...] = jnp.max(final_acc[...].T, 0, keepdims=True)[0, :OWN]
 
     @pl.when(jnp.logical_not(inner))
     def _():
@@ -385,9 +403,9 @@
             copy(1, 5, 3, k, sister).wait_send()
 
             copy(0, 6, 4, k, across).wait_send()
-            copy(1, 7, 5, k, across).wait_send()
-            copy(6, 8, 6, k, sister).wait_send()
-            copy(7, 9, 7, k, sister).wait_send()
+            copy(1, 8, 5, k, across).wait_send()
+            copy(6, 7, 6, k, sister).wait_send()
+            copy(8, 9, 7, k, sister).wait_send()
 
         for step in range(1, 16):
             place_copy(step, (me + step) % 16, rank).wait_send()
@@ -401,21 +419,21 @@
     pieces = 3
     size = -(-sent // (16 * pieces)) * 16
     chunks = [(begin, min(size, sent - begin)) for begin in range(0, sent, size)]
-    slot_index = jnp.arange(padded)
-    place = jnp.where(
-        slot_index < shard_count[0], jnp.pad(row_position, (0, padded - capacity)), -1
-    )[None, :]
     tall = -(-OWN // LANES) * LANES
-    found = pl.pallas_call(
+    return pl.pallas_call(
         functools.partial(line_kernel, capacity, sent, padded, chunks),
-        out_shape=jax.ShapeDtypeStruct((1, tall), jnp.float32),
-        in_specs=[pl.BlockSpec(memory_space=pltpu.VMEM)] * 2,
+        out_shape=jax.ShapeDtypeStruct((OWN,), jnp.float32),
+        in_specs=[
+            pl.BlockSpec(memory_space=pltpu.VMEM),
+            pl.BlockSpec(memory_space=pltpu.VMEM),
+            pl.BlockSpec(memory_space=pltpu.SMEM),
+        ],
         out_specs=pl.BlockSpec(memory_space=pltpu.VMEM),
         scratch_shapes=[
             pltpu.VMEM((SLOTS, padded, feature), jnp.bfloat16),
             pltpu.VMEM((SLOTS, 1, padded), jnp.int32),
             pltpu.VMEM((8, 2, 1, padded), jnp.int32),
-            pltpu.VMEM((4, padded, LANES), jnp.float32),
+            pltpu.VMEM((8, padded, LANES), jnp.float32),
             pltpu.VMEM((SLOTS, 8, padded), jnp.float32),
             pltpu.VMEM((SLOTS, padded, LANES), jnp.float32),
             pltpu.VMEM((SLOTS, 1, padded), jnp.float32),
@@ -430,8 +448,7 @@
             pltpu.SemaphoreType.DMA((8,)),
         ],
         compiler_params=pltpu.CompilerParams(collective_id=0, has_side_effects=True),
-    )(shard_rows, place)
-    return found[0, :OWN]
+    )(shard_rows, row_position, shard_count)
 
 
 def solution(mesh):

time: 36.3 us -> 35.1 us (0.967)
  Pallas kernels: 33.7 us -> 33 us
  local copies, waits for them, and re-layouts: 1.8 us -> 1.24 us
    pallas_call x1, Pallas kernels: 33.7 us -> 33 us  [line_body(): pl.pallas_call(functools.partial(line_kernel, capacity, sent, padded, chu...]
    broadcast_in_dim x1 -> x0, local copies, waits for them, and re-layouts: 0.56 us -> none  [line_body(): jnp.where(slot_index < shard_count[0], jnp.pad(row_position, (0, padded -...]
    unnamed x5 -> x1, local copies, waits for them, and re-layouts: 1.24 us -> 1.24 us
where the time goes in v3:
time: 35.1 us; the launch traced here: 34.9 us
  Pallas kernels  33 us (94%)
  local copies, waits for them, and re-layouts  1.24 us (4%)
  between operations  0.66 us (2%)
    pallas_call x1, Pallas kernels, line_body(): pl.pallas_call(functools.partial(line_kernel, capacity, sent, padded, chu...  33 us
    unnamed x1, local copies, waits for them, and re-layouts  1.24 us

profile of v3, /device:TPU:0, one launch (start us, length us, event | category | flops | bytes accessed | tf_op | source)
XLA Modules:
  0.0 34.9 jit_solution(10278516760345582729)
XLA Ops:
  0.7 33.0 %shard_map.37 = f32[192]{0:T(256)} custom-call(bf16[360,512]{1,0:T(8,128)(2,1)} %rows_ref.1, s32[360]{0:T(512)} %raw_ref.1, s32[1]{0:T(128)S(6)} %copy.5.count_ref), custom_call_target="tpu_custom_call" | custom-call | tf_op jit(solution)/shard_map/pallas_call | solution.py:423
  33.7 1.2 %copy.6 = f32[192]{0:T(256)} copy(f32[192]{0:T(256)} %shard_map.37) | data formatting | bytes 1536
